TPU v7x, 32 devices: a whole 2x2x4 slice. The times are simulated.
32 devices in a mesh: dp: 4 (over y, x), expert: 8 (over z, core).
Axes of the slice: x: 2, y: 2, z: 4, core: 2. Of those that a mesh axis runs over, the one named last changes fastest.
Arguments:
- tables: float32 [4, 8192, 256], P(None, ('dp', 'expert')), may hold values from -3 to 3
- accum: float32 [4, 8192], P(None, ('dp', 'expert')), may hold values from 0.01 to 1
- bag_owner: int32 [4096, 16], P(('dp', 'expert')), may hold values from 0 to 31, all different within a row; in each aligned block of 128 rows (0 to 127, 128 to 255, ...) at most 81 rows name the same one
- bag_row: int32 [4096, 16], P(('dp', 'expert')), may hold values from 0 to 255
- bag_len: int32 [4, 4096], P(None, ('dp', 'expert')), may hold values from 1 to 4, 10240 in all within a row
- route: int32 [4096, 2], P(('dp', 'expert')), may hold values from 0 to 7, all different within a row; in each aligned block of 128 rows (0 to 127, 128 to 255, ...) at most 33 rows name the same one
- labels: float32 [4096, 2], P(('dp', 'expert')), may hold values from 0 to 1
- w_in: bfloat16 [8, 1024, 2048], P('expert', None, 'dp'), may hold values from -0.1875 to 0.1875
- w_out: bfloat16 [8, 2048, 1024], P('expert', 'dp'), may hold values from -0.125 to 0.125
- gate_w: bfloat16 [2, 1024, 8], replicated, may hold values from -0.1875 to 0.1875
- head: float32 [2, 1024], replicated, may hold values from -0.375 to 0.375
Outputs:
- logits: float32 [4096, 2], P(('dp', 'expert'))
- new_tables: float32 [4, 8192, 256], P(None, ('dp', 'expert'))
- new_accum: float32 [4, 8192], P(None, ('dp', 'expert'))
Inputs may be any that keep to these rules, and one draw needn't show every extreme that they name: `bag_owner`: each sample names 16 different owners; the rows of one device name any one owner at most 81 times. `route`: each sample names two different experts; the rows of one device name any one expert at most 33 times.
All inputs are finite; a program needn't handle non-finite values. No bound on the sum of `bag_len` on one device may be relied on, other than what follows from the above.
Results may differ from a plain program's by a relative error of at most 0.0062.
Values may be sent and summed in bfloat16 or wider, within the bound.
No kernel may reach another device: no remote copies, remote signals or barrier semaphores. Data moves between devices by JAX's collectives and lax.ppermute only.
A program may use at most 128 MiB of HBM per device.

v0:
```python
import jax
import jax.numpy as jnp
from jax import lax
from jax.sharding import PartitionSpec as P

learn_rate = 0.3
norm_eps = 1e-05


def slot_rank(dest, buckets):
    count = dest.shape[0]
    order = jnp.argsort(dest, stable=True)
    ordered = dest[order]
    starts = jnp.searchsorted(ordered, jnp.arange(buckets, dtype=jnp.int32), side="left")
    within = jnp.arange(count, dtype=jnp.int32) - starts[ordered]
    return jnp.zeros((count,), jnp.int32).at[order].set(within)


def send_requests(requests):
    return lax.all_to_all(
        lax.all_to_all(requests, "expert", split_axis=2, concat_axis=2, tiled=True),
        "dp",
        split_axis=1,
        concat_axis=1,
        tiled=True,
    )


def send_rows(values):
    return lax.all_to_all(
        lax.all_to_all(values, "expert", split_axis=2, concat_axis=2, tiled=True),
        "dp",
        split_axis=1,
        concat_axis=1,
        tiled=True,
    )


def per_device(
    tables, accum, bag_owner, bag_row, bag_len, route, labels, w_in, w_out, gate_w, head
):
    dp_count = lax.axis_size("dp")
    expert_count = lax.axis_size("expert")
    device_count = dp_count * expert_count
    sample_count = route.shape[0]
    table_count = tables.shape[0]
    row_count = tables.shape[1]
    emb_width = tables.shape[2]
    bag_slots = bag_owner.shape[1] // table_count
    model_width = table_count * emb_width
    task_count = labels.shape[1]
    cap_rows = (5 * sample_count * table_count * bag_slots + 4 * device_count - 1) // (
        4 * device_count
    ) + 1
    cap_expert = (2 * sample_count + expert_count - 1) // expert_count + 1
    full_in, full_out = (
        lax.all_gather(w_in[0], "dp", axis=1, tiled=True),
        lax.all_gather(w_out[0], "dp", axis=0, tiled=True),
    )
    lookups = sample_count * table_count * bag_slots
    owners = bag_owner.reshape(-1)
    column = jnp.arange(lookups, dtype=jnp.int32) % (table_count * bag_slots)
    table_of = column // bag_slots
    owner_slot = slot_rank(owners, device_count)
    flat_row = table_of * row_count + bag_row.reshape(-1)
    requests = jnp.zeros((cap_rows, device_count), jnp.int32).at[owner_slot, owners].set(flat_row)
    wanted = send_requests(requests.reshape(cap_rows, dp_count, expert_count))
    flat_table = tables.reshape(table_count * row_count, emb_width)
    served = flat_table[wanted.reshape(-1)].reshape(cap_rows, dp_count, expert_count, emb_width)
    returned = send_rows(served).reshape(cap_rows * device_count, emb_width)
    fetched = returned[owner_slot * device_count + owners]
    live = (jnp.arange(bag_slots, dtype=jnp.int32)[None, None, :] < bag_len.T[:, :, None]).reshape(
        -1
    )
    masked = jnp.where(live[:, None], fetched, 0.0)
    pooled = jnp.sum(masked.reshape(sample_count, table_count, bag_slots, emb_width), axis=2)
    features = pooled.reshape(sample_count, model_width).astype(jnp.bfloat16)
    experts_flat = route.reshape(-1)
    expert_slot = slot_rank(experts_flat, expert_count)
    sample_of = jnp.arange(2 * sample_count, dtype=jnp.int32) // 2
    outgoing = (
        jnp.zeros((cap_expert, expert_count, model_width), jnp.bfloat16)
        .at[expert_slot, experts_flat]
        .set(features[sample_of])
    )
    arrived = lax.all_to_all(outgoing, "expert", split_axis=1, concat_axis=1, tiled=True)
    flat = arrived.reshape(-1, model_width)
    pre = jnp.dot(flat, full_in, preferred_element_type=jnp.float32)
    hidden = jnp.maximum(pre, 0.0).astype(jnp.bfloat16)
    result = jnp.dot(hidden, full_out, preferred_element_type=jnp.float32).astype(jnp.bfloat16)
    result = result.reshape(arrived.shape)
    saved_part = hidden.reshape(arrived.shape[0], arrived.shape[1], hidden.shape[1])
    back = lax.all_to_all(result, "expert", split_axis=1, concat_axis=1, tiled=True)
    picked = (
        back[expert_slot, experts_flat].reshape(sample_count, 2, model_width).astype(jnp.float32)
    )
    scores = jnp.einsum("sd,tde->ste", features, gate_w, preferred_element_type=jnp.float32)
    chosen = jnp.take_along_axis(
        scores, jnp.broadcast_to(route[:, None, :], (sample_count, task_count, 2)), axis=2
    )
    first = jax.nn.sigmoid(chosen[..., 0] - chosen[..., 1])
    gates = jnp.stack([first, 1.0 - first], axis=-1)
    combined = jnp.einsum("stk,skd->std", gates, picked, precision=lax.Precision.HIGHEST)
    scale = jnp.sqrt(jnp.mean(combined * combined, axis=-1, keepdims=True) + norm_eps)
    normed = combined / scale
    logits = jnp.sum(normed * head[None], axis=-1)
    dlogit = jax.nn.sigmoid(logits) - labels
    dnormed = dlogit[..., None] * head[None]
    dcomb = (dnormed - normed * jnp.mean(dnormed * normed, axis=-1, keepdims=True)) / scale
    dpicked = jnp.einsum("stk,std->skd", gates, dcomb, precision=lax.Precision.HIGHEST).astype(
        jnp.bfloat16
    )
    dgates = jnp.einsum("std,skd->stk", dcomb, picked, precision=lax.Precision.HIGHEST)
    ddelta = (dgates[..., 0] - dgates[..., 1]) * first * (1.0 - first)
    onehot = (route[:, :, None] == jnp.arange(expert_count, dtype=jnp.int32)[None, None, :]).astype(
        jnp.float32
    )
    dscores = ddelta[:, :, None] * (onehot[:, None, 0, :] - onehot[:, None, 1, :])
    dgate_in = jnp.einsum(
        "ste,tde->sd", dscores, gate_w.astype(jnp.float32), precision=lax.Precision.HIGHEST
    )
    grads_out = (
        jnp.zeros((cap_expert, expert_count, model_width), jnp.bfloat16)
        .at[expert_slot, experts_flat]
        .set(dpicked.reshape(-1, model_width))
    )
    arrived_grads = lax.all_to_all(grads_out, "expert", split_axis=1, concat_axis=1, tiled=True)
    flat_grads = arrived_grads.reshape(-1, model_width)
    dhidden = lax.dot_general(
        flat_grads, full_out, (((1,), (1,)), ((), ())), preferred_element_type=jnp.float32
    )
    active = saved_part.reshape(-1, full_in.shape[1]) > 0
    dpre = jnp.where(active, dhidden, 0.0).astype(jnp.bfloat16)
    dinput = lax.dot_general(
        dpre, full_in, (((1,), (1,)), ((), ())), preferred_element_type=jnp.float32
    )
    dinput = dinput.astype(jnp.bfloat16).reshape(arrived_grads.shape)
    back_grads = lax.all_to_all(dinput, "expert", split_axis=1, concat_axis=1, tiled=True)
    dexpert = (
        back_grads[expert_slot, experts_flat]
        .astype(jnp.float32)
        .reshape(sample_count, 2, model_width)
    )
    dfeatures = dgate_in + jnp.sum(dexpert, axis=1)
    dpooled = dfeatures.reshape(sample_count, table_count, emb_width)
    per_lookup = jnp.broadcast_to(
        dpooled[:, :, None, :], (sample_count, table_count, bag_slots, emb_width)
    ).reshape(lookups, emb_width)
    per_lookup = jnp.where(live[:, None], per_lookup, 0.0)
    grad_buffer = (
        jnp.zeros((cap_rows, device_count, emb_width), jnp.float32)
        .at[owner_slot, owners]
        .set(per_lookup)
    )
    arrived_rows = send_rows(grad_buffer.reshape(cap_rows, dp_count, expert_count, emb_width))
    row_grads = (
        jnp.zeros((table_count * row_count, emb_width), jnp.float32)
        .at[wanted.reshape(-1)]
        .add(arrived_rows.reshape(-1, emb_width))
    )
    row_grads = row_grads.reshape(table_count, row_count, emb_width)
    new_accum = accum + jnp.mean(row_grads * row_grads, axis=-1)
    new_tables = tables - learn_rate * row_grads / jnp.sqrt(new_accum)[..., None]
    return (logits, new_tables, new_accum)


def solution(mesh):
    in_specs = (
        P(None, ("dp", "expert"), None),
        P(None, ("dp", "expert")),
        P(("dp", "expert"), None),
        P(("dp", "expert"), None),
        P(None, ("dp", "expert")),
        P(("dp", "expert"), None),
        P(("dp", "expert"), None),
        P("expert", None, "dp"),
        P("expert", "dp", None),
        P(),
        P(),
    )
    out_specs = (
        P(("dp", "expert"), None),
        P(None, ("dp", "expert"), None),
        P(None, ("dp", "expert")),
    )
    return jax.shard_map(
        per_device, mesh=mesh, in_specs=in_specs, out_specs=out_specs, check_vma=False
    )
```

profile of v0, /device:TPU:0, one launch (start us, length us, event | category | flops | bytes accessed | tf_op | source)
XLA Modules:
  0.0 530.2 jit_solution(621122116833927265)
XLA Ops:
  8.8 5.0 sort.34
  13.9 11.8 %gather_fusion.2 = s32[2048]{0:T(1024)S(1)} fusion(s32[2048]{0:T(1024)S(1)} %reshape.277, s32[2048]{0:T(1024)S(1)} %get-tuple-element.251), kind=kCustom, calls=%fused_computation.2 | custom fusion | bytes 24576 | tf_op jit(solution)/shard_map/gather | solution.py:13
  25.7 9.0 %while.48 = (s32[]{:T(128)}, u32[32]{0:T(128)S(1)}, u32[32]{0:T(128)S(1)}, s32[2048]{0:T(1024)S(1)}, s32[]{:T(128)}, /*index=5*/s32[]{:T(128)}, s32[]{}) while((s32[]{:T(128)}, u32[32]{0:T(128)S(1)}, u32[32]{0:T(128)S(1)}, s32[2048]{0:T(1024)S(1)}, s32[]{:T(128)}, /*index=5*/s32[]{:T(128)}, s32[]{}) %tuple.144), condition=%wide.region_2.3_spmd.clone, body=%wide.region_1.2_spmd.clone.sunk | while | flops 1444 | bytes 5732 | solution.py:14
  41.4 15.6 %select_subtract_fusion = s32[2048]{0:T(1024)S(1)} fusion(pred[2048]{0:T(1024)(128)(4,1)S(1)} %get-tuple-element.214, pred[2048]{0:T(1024)(128)(4,1)S(1)} %get-tuple-element.213, pred[2048]{0:T(1024)(128)(4,1)S(1)} %get-tuple-element.212, pred[2048]{0:T(1024)(128)(4,1)S(1)} %get-tuple-element.211, pred[2048]{0:T(1024)(128)(4,1)S(1)} %get-tuple-element.210, ...), kind=kLoop, calls=%fused_computation.132 | loop fusion | flops 53248 | bytes 67684 | tf_op jit(solution)/shard_map/sub | solution.py:15
  57.0 8.0 %scatter_custom_fusion = s32[2048]{0:T(1024)S(1)} fusion(s32[2048]{0:T(1024)S(1)} %get-tuple-element.252, s32[2048]{0:T(1024)S(1)} %select_subtract_fusion, s32[]{:T(128)} %constant.134.clone.1), kind=kCustom, calls=%fused_computation.157 | custom fusion | bytes 8196 | tf_op jit(solution)/shard_map/scatter | solution.py:16
  65.9 8.1 %scatter_custom_fusion.5 = s32[2592]{0:T(1024)S(1)} fusion(s32[2048]{0:T(1024)S(1)} %get-tuple-element.254, s32[2048]{0:T(1024)S(1)} %get-tuple-element.297, s32[]{:T(128)} %constant.134.clone.1), kind=kCustom, calls=%fused_computation.143 | custom fusion | bytes 10372
  74.1 11.8 %all_to_all.50 = s32[81,4,8]{0,1,2:T(4,128)S(1)} all-to-all(s32[81,4,8]{0,1,2:T(4,128)S(1)} %copy.196), channel_id=1, replica_groups=mesh['dp'=4,'expert'=8] {'expert'}, dimensions={2} | all-to-all | bytes 20736 | tf_op jit(solution)/shard_map/all_to_all | solution.py:21
  85.9 8.2 %all_to_all.51 = s32[81,4,8]{0,2,1:T(8,128)S(1)} all-to-all(s32[81,4,8]{0,2,1:T(8,128)S(1)} %copy.197), channel_id=1, replica_groups=mesh['dp'=4,'expert'=8] {'dp'}, dimensions={1} | all-to-all | bytes 20736 | tf_op jit(solution)/shard_map/all_to_all | solution.py:20
  94.5 7.6 %gather_fusion.3 = f32[2592,256]{1,0:T(8,128)} fusion(f32[1024,256]{1,0:T(8,128)S(1)} %bitcast.129, s32[3072]{0:T(1024)S(1)} %pad_clamp_fusion.2), kind=kCustom, calls=%fused_computation.3 | custom fusion | bytes 5318784 | tf_op jit(solution)/shard_map/gather | solution.py:69
  117.2 54.8 %all-to-all-done.2 = f32[81,4,8,256]{3,1,0,2:T(4,128)} async-done(((f32[81,4,8,256]{3,1,0,2:T(4,128)}), f32[81,4,8,256]{3,1,0,2:T(4,128)}, u32[]{:S(2)}, u32[]{:S(2)}) %all-to-all-start.2) | async-done | bytes 2654240 | tf_op jit(solution)/shard_map/all_to_all | solution.py:31
  180.5 6.3 %while.49 = (s32[]{:T(128)}, u32[8]{0:T(128)S(1)}, u32[8]{0:T(128)S(1)}, s32[256]{0:T(256)S(1)}, s32[]{:T(128)}, /*index=5*/s32[]{:T(128)}, s32[]{}) while((s32[]{:T(128)}, u32[8]{0:T(128)S(1)}, u32[8]{0:T(128)S(1)}, s32[256]{0:T(256)S(1)}, s32[]{:T(128)}, /*index=5*/s32[]{:T(128)}, s32[]{}) %tuple.147), condition=%wide.region_8.9_spmd.clone, body=%wide.region_7.8_spmd.clone.sunk | while | flops 1132 | bytes 4580 | solution.py:14
  195.0 16.4 %all-to-all-done.3 = f32[81,4,8,256]{3,2,0,1:T(8,128)} async-done(((f32[81,4,8,256]{3,2,0,1:T(8,128)}), f32[81,4,8,256]{3,2,0,1:T(8,128)}, u32[]{:S(2)}, u32[]{:S(2)}) %all-to-all-start.3) | async-done | bytes 2654240 | tf_op jit(solution)/shard_map/all_to_all | solution.py:30
  215.1 8.4 %gather_fusion.4 = f32[2048,256]{1,0:T(8,128)S(1)} fusion(f32[2592,256]{1,0:T(8,128)} %bitcast.130, s32[2048]{0:T(1024)S(1)} %get-tuple-element.249), kind=kCustom, calls=%fused_computation.4 | custom fusion | bytes 4202496 | tf_op jit(solution)/shard_map/gather | solution.py:71
  229.5 16.0 %scatter_fusion = bf16[33,8,1024]{2,1,0:T(8,128)(2,1)S(1)} fusion(bf16[33,8,1024]{2,1,0:T(8,128)(2,1)S(1)} %broadcast.283.clone, s32[256]{0:T(256)S(1)} %bitcast.133, bf16[256,1024]{1,0:T(8,128)(2,1)S(1)} %gather_fusion.6), kind=kCustom, calls=%fused_computation.12 | custom fusion | bytes 1574912 | tf_op jit(solution)/shard_map/scatter | solution.py:84
  250.2 18.0 %all-to-all-done.4 = bf16[33,8,1024]{2,0,1:T(8,128)(2,1)S(1)} async-done(((bf16[33,8,1024]{2,0,1:T(8,128)(2,1)}), bf16[33,8,1024]{2,0,1:T(8,128)(2,1)S(1)}, u32[]{:S(2)}, u32[]{:S(2)}) %all-to-all-start.4) | async-done | bytes 540704 | tf_op jit(solution)/shard_map/all_to_all | solution.py:86
  285.1 13.6 %all-to-all-done.5 = bf16[33,8,1024]{2,0,1:T(8,128)(2,1)S(1)} async-done(((bf16[33,8,1024]{2,0,1:T(8,128)(2,1)}), bf16[33,8,1024]{2,0,1:T(8,128)(2,1)S(1)}, u32[]{:S(2)}, u32[]{:S(2)}) %all-to-all-start.5) | async-done | bytes 540704 | tf_op jit(solution)/shard_map/all_to_all | solution.py:93
  311.8 16.0 %scatter_fusion.1 = bf16[33,8,1024]{2,1,0:T(8,128)(2,1)S(1)} fusion(bf16[33,8,1024]{2,1,0:T(8,128)(2,1)S(1)} %broadcast.283, s32[256]{0:T(256)S(1)} %bitcast.134, bf16[256,1024]{1,0:T(8,128)(2,1)S(1)} %reshape.457), kind=kCustom, calls=%fused_computation.13 | custom fusion | bytes 1574912 | tf_op jit(solution)/shard_map/scatter | solution.py:125
  332.7 17.8 %all-to-all-done.6 = bf16[33,8,1024]{2,0,1:T(8,128)(2,1)S(1)} async-done(((bf16[33,8,1024]{2,0,1:T(8,128)(2,1)}), bf16[33,8,1024]{2,0,1:T(8,128)(2,1)S(1)}, u32[]{:S(2)}, u32[]{:S(2)}) %all-to-all-start.6) | async-done | bytes 540704 | tf_op jit(solution)/shard_map/all_to_all | solution.py:127
  350.5 6.4 %fusion.40 = bf16[33,8,1024]{2,1,0:T(8,128)(2,1)S(1)} fusion(bf16[1,1024,2048]{2,1,0:T(8,128)(2,1)} %all-gather.5.cloned.1.call-done, bf16[1,2048,1024]{2,1,0:T(8,128)(2,1)} %all-gather.7.cloned.1.call-done, bf16[264,2048]{1,0:T(8,128)(2,1)} %copy-done.13, bf16[33,8,1024]{2,0,1:T(8,128)(2,1)S(1)} %all-to-all-done.6), kind=kOutput, calls=%fused_computation.55 | convolution fusion | flops 2216484864 | bytes 10551296 | tf_op jit(solution)/shard_map/dot_general | solution.py:134
  367.2 12.7 %all-to-all-done.7 = bf16[33,8,1024]{2,0,1:T(8,128)(2,1)S(1)} async-done(((bf16[33,8,1024]{2,0,1:T(8,128)(2,1)}), bf16[33,8,1024]{2,0,1:T(8,128)(2,1)S(1)}, u32[]{:S(2)}, u32[]{:S(2)}) %all-to-all-start.7) | async-done | bytes 540704 | tf_op jit(solution)/shard_map/all_to_all | solution.py:138
  389.5 12.2 %scatter_custom_fusion.6 = f32[2592,256]{1,0:T(8,128)} fusion(s32[2048]{0:T(1024)} %get-tuple-element.253, f32[2048,256]{1,0:T(8,128)S(1)} %reshape.292, f32[]{:T(128)} %constant.151.clone.1, pred[2048]{0:T(1024)(128)(4,1)S(1)} %lt.149), kind=kCustom, calls=%fused_computation.45 | custom fusion | flops 524288 | bytes 4754432
  404.4 63.4 %all_to_all.52 = f32[81,4,8,256]{3,1,0,2:T(4,128)S(1)} all-to-all(f32[81,4,8,256]{3,1,0,2:T(4,128)S(1)} %copy.220), channel_id=1, replica_groups=mesh['dp'=4,'expert'=8] {'expert'}, dimensions={2} | all-to-all | bytes 5308416 | tf_op jit(solution)/shard_map/all_to_all | solution.py:31
  468.3 34.5 %all_to_all.53 = f32[81,4,8,256]{3,2,0,1:T(8,128)S(1)} all-to-all(f32[81,4,8,256]{3,2,0,1:T(8,128)S(1)} %copy.221), channel_id=1, replica_groups=mesh['dp'=4,'expert'=8] {'dp'}, dimensions={1} | all-to-all | bytes 5308416 | tf_op jit(solution)/shard_map/all_to_all | solution.py:30
  504.7 16.1 %scatter_custom_fusion.4 = f32[1024,256]{1,0:T(8,128)S(1)} fusion(s32[2592]{0:T(1024)S(1)} %fusion.60, f32[2592,256]{1,0:T(8,128)} %bitcast.140, f32[]{:T(128)} %constant.151.clone.1), kind=kCustom, calls=%fused_computation.73 | custom fusion | flops 663552 | bytes 1049088 | tf_op jit(solution)/shard_map/scatter-add | solution.py:159
  (238 shorter events, 132.0 us)
Async XLA Ops:
  7.2 273.9 %copy-start = (bf16[2,1024,8]{1,2,0:T(8,128)(2,1)S(1)}, bf16[2,1024,8]{1,2,0:T(8,128)(2,1)}, u32[]{:S(2)}) copy-start(bf16[2,1024,8]{1,2,0:T(8,128)(2,1)} %param.24) | copy-start | bytes 98308
  7.2 243.0 %all-gather.5.cloned.1.call-start = ((), (), s32[]{:S(2)}) async-start(), calls=%async_computation.10 | async-start | bytes 5242880 | tf_op jit(solution)/shard_map/all_gather | solution.py:57
  13.9 26.0 %copy-start.5 = (s32[128,16]{0,1:T(8,128)S(1)}, s32[128,16]{0,1:T(8,128)}, u32[]{:S(2)}) copy-start(s32[128,16]{0,1:T(8,128)} %param.18) | copy-start | bytes 24580
  25.7 39.4 %copy-start.12 = (s32[2]{0:T(128)S(1)}, s32[2]{0:T(128)}, u32[]{:S(2)}) copy-start(s32[2]{0:T(128)} %constant.166) | copy-start | bytes 28
  25.7 39.5 %copy-start.10 = (s32[2]{0:T(128)S(1)}, s32[2]{0:T(128)}, u32[]{:S(2)}) copy-start(s32[2]{0:T(128)} %constant.163) | copy-start | bytes 28
  25.7 39.5 %copy-start.11 = (s32[2]{0:T(128)S(1)}, s32[2]{0:T(128)}, u32[]{:S(2)}) copy-start(s32[2]{0:T(128)} %constant.169) | copy-start | bytes 28
  25.7 68.8 %copy-start.1 = (f32[4,256,256]{2,1,0:T(8,128)S(1)}, f32[4,256,256]{2,1,0:T(8,128)}, u32[]{:S(2)}) copy-start(f32[4,256,256]{2,1,0:T(8,128)} %param.15) | copy-start | bytes 3145732
  106.5 5.3 %copy-start.4 = (s32[128,2]{0,1:T(2,128)S(1)}, s32[128,2]{0,1:T(2,128)}, u32[]{:S(2)}) copy-start(s32[128,2]{0,1:T(2,128)} %param.20) | copy-start | bytes 3076
  106.5 65.5 %all-to-all-start.2 = ((f32[81,4,8,256]{3,1,0,2:T(4,128)}), f32[81,4,8,256]{3,1,0,2:T(4,128)}, u32[]{:S(2)}, u32[]{:S(2)}) async-start(f32[81,4,8,256]{3,1,0,2:T(4,128)} %copy.199), calls=%async_computation.2 | async-start | bytes 5308416 | tf_op jit(solution)/shard_map/all_to_all | solution.py:31
  111.1 160.9 %all-gather.7.cloned.1.call-start = ((), (), s32[]{:S(2)}) async-start(), calls=%async_computation.11 | async-start | bytes 5242880 | tf_op jit(solution)/shard_map/all_gather | solution.py:58
  175.9 35.5 %all-to-all-start.3 = ((f32[81,4,8,256]{3,2,0,1:T(8,128)}), f32[81,4,8,256]{3,2,0,1:T(8,128)}, u32[]{:S(2)}, u32[]{:S(2)}) async-start(f32[81,4,8,256]{3,2,0,1:T(8,128)} %copy.200), calls=%async_computation.3 | async-start | bytes 5308416 | tf_op jit(solution)/shard_map/all_to_all | solution.py:30
  180.5 6.5 %copy-start.8 = (s32[4,128]{1,0:T(4,128)S(1)}, s32[4,128]{1,0:T(4,128)}, u32[]{:S(2)}) copy-start(s32[4,128]{1,0:T(4,128)} %param.19) | copy-start | bytes 6148
  246.6 21.6 %all-to-all-start.4 = ((bf16[33,8,1024]{2,0,1:T(8,128)(2,1)}), bf16[33,8,1024]{2,0,1:T(8,128)(2,1)S(1)}, u32[]{:S(2)}, u32[]{:S(2)}) async-start(bf16[33,8,1024]{2,0,1:T(8,128)(2,1)} %copy.206), calls=%async_computation.4 | async-start | bytes 1310720 | tf_op jit(solution)/shard_map/all_to_all | solution.py:86
  271.9 3.9 copy-start.13
  277.0 21.8 %all-to-all-start.5 = ((bf16[33,8,1024]{2,0,1:T(8,128)(2,1)}), bf16[33,8,1024]{2,0,1:T(8,128)(2,1)S(1)}, u32[]{:S(2)}, u32[]{:S(2)}) async-start(bf16[33,8,1024]{2,0,1:T(8,128)(2,1)} %copy.208), calls=%async_computation.5 | async-start | bytes 1310720 | tf_op jit(solution)/shard_map/all_to_all | solution.py:93
  301.7 3.0 copy-start.3
  301.9 2.8 copy-start.2
  302.0 3.6 copy-start.9
  305.6 0.6 copy-start.6
  328.9 21.6 %all-to-all-start.6 = ((bf16[33,8,1024]{2,0,1:T(8,128)(2,1)}), bf16[33,8,1024]{2,0,1:T(8,128)(2,1)S(1)}, u32[]{:S(2)}, u32[]{:S(2)}) async-start(bf16[33,8,1024]{2,0,1:T(8,128)(2,1)} %copy.216), calls=%async_computation.6 | async-start | bytes 1310720 | tf_op jit(solution)/shard_map/all_to_all | solution.py:127
  358.1 21.8 %all-to-all-start.7 = ((bf16[33,8,1024]{2,0,1:T(8,128)(2,1)}), bf16[33,8,1024]{2,0,1:T(8,128)(2,1)S(1)}, u32[]{:S(2)}, u32[]{:S(2)}) async-start(bf16[33,8,1024]{2,0,1:T(8,128)(2,1)} %copy.218), calls=%async_computation.7 | async-start | bytes 1310720 | tf_op jit(solution)/shard_map/all_to_all | solution.py:138
  504.7 16.4 %copy-start.7 = (f32[4,256]{1,0:T(4,128)S(1)}, f32[4,256]{1,0:T(4,128)}, u32[]{:S(2)}) copy-start(f32[4,256]{1,0:T(4,128)} %param.16) | copy-start | bytes 12292
Sparse Core Ops, SparseCore 0:
  9.8 55.1 all-gather.4
  113.7 52.0 all-gather.6
where the time goes:
time: 539 us; the launch traced here: 530 us
  local copies, waits for them, and re-layouts  140 us (26%)
  waiting for transfers between devices  135 us (25%)
  blocking collectives  118 us (22%)
  other arithmetic  72.4 us (13%)
  matrix products  26 us (5%)
  starting transfers between devices  23.8 us (4%)
  between operations  15.3 us (3%)
    all_to_all x1, blocking collectives, send_rows(): lax.all_to_all(values, 'expert', split_axis=2, concat_axis=2, tiled=True)  63.4 us
    all_to_all x1, waiting for transfers between devices, send_rows(): lax.all_to_all(values, 'expert', split_axis=2, concat_axis=2, tiled=True)  54.8 us
    all_to_all x1, blocking collectives, send_rows(): lax.all_to_all(lax.all_to_all(values, 'expert', split_axis=2, concat_axis...  34.5 us
    all_to_all x1, waiting for transfers between devices, per_device(): lax.all_to_all(outgoing, 'expert', split_axis=1, concat_axis=1, tiled=True)  18 us
    all_to_all x1, waiting for transfers between devices, per_device(): lax.all_to_all(grads_out, 'expert', split_axis=1, concat_axis=1, tiled=True)  17.8 us
    scatter x2, local copies, waits for them, and re-layouts, per_device(): grads_out = jnp.zeros((cap_expert, expert_count, model_width), jnp.bfloat...  17.1 us
    scatter x2, local copies, waits for them, and re-layouts, per_device(): outgoing = jnp.zeros((cap_expert, expert_count, model_width), jnp.bfloat1...  17.1 us
    all_to_all x1, waiting for transfers between devices, send_rows(): lax.all_to_all(lax.all_to_all(values, 'expert', split_axis=2, concat_axis...  16.4 us
  transfers between devices with their start and end apart: 8, of which 6 were waited for; matrix products, arithmetic and copies ran while one was open for 28% of the time, Pallas kernels for 0%

commit v1 on v0

--- a/solution.py
+++ b/solution.py
@@ -2,6 +2,7 @@
 import jax.numpy as jnp
 from jax import lax
 from jax.sharding import PartitionSpec as P
+from jax.lax import all_to_all, axis_size
 
 learn_rate = 0.3
 norm_eps = 1e-05
@@ -27,12 +28,16 @@
 
 
 def send_rows(values):
+
+    def desk_derive(buf, bus_axis):
+        u_next = axis_size(bus_axis)
+        outcome_arr = jnp.split(buf, u_next, axis=2)
+        x_new = jnp.stack(outcome_arr)
+        small = all_to_all(x_new, axis_name=bus_axis, split_axis=0, concat_axis=0)
+        return jnp.concatenate(small, axis=2)
+
     return lax.all_to_all(
-        lax.all_to_all(values, "expert", split_axis=2, concat_axis=2, tiled=True),
-        "dp",
-        split_axis=1,
-        concat_axis=1,
-        tiled=True,
+        desk_derive(values, "expert"), "dp", split_axis=1, concat_axis=1, tiled=True
     )
 
 

time: 539 us -> 563 us (1.045)
  local copies, waits for them, and re-layouts: 140 us -> 175 us
  waiting for transfers between devices: 135 us -> 126 us
  blocking collectives: 118 us -> 110 us
    unnamed x37 -> x57, local copies, waits for them, and re-layouts: 9.93 us -> 25.7 us
    scatter x2, local copies, waits for them, and re-layouts: 9.97 us -> 23.3 us  [slot_rank(): return jnp.zeros((count,), jnp.int32).at[order].set(within)]
    split x0 -> x1, local copies, waits for them, and re-layouts: none -> 10.7 us  [desk_derive(): outcome_arr = jnp.split(buf, u_next, axis=2)]
    all_to_all x3 -> x2, blocking collectives: 106 us -> 97.9 us  [the longest x1 63.4 us: desk_derive(): small = all_to_all(x_new, axis_name=bus_axis, split_axis=0, concat_axis=0)]
    all_to_all x2 -> x3, waiting for transfers between devices: 71.2 us -> 63.5 us  [the longest x1 54.8 us: desk_derive(): small = all_to_all(x_new, axis_name=bus_axis, split_axis=0, concat_axis=0)]
    all_to_all x2 -> x3, starting transfers between devices: 9.17 us -> 12.9 us  [the longest x1 4.61 us: send_rows(): lax.all_to_all(desk_derive(values, 'expert'), 'dp', split_axis=1, concat_...]
  transfers between devices with their start and end apart: 8 -> 9, of which waited for: 6 -> 7; matrix products, arithmetic and copies ran while one was open for 28% -> 20% of each run, Pallas kernels for 0% -> 0%
where the time goes in v1:
time: 563 us; the launch traced here: 553 us
  local copies, waits for them, and re-layouts  175 us (31%)
  waiting for transfers between devices  126 us (22%)
  blocking collectives  110 us (20%)
  other arithmetic  72.6 us (13%)
  starting transfers between devices  28.5 us (5%)
  matrix products  25.9 us (5%)
  between operations  15.2 us (3%)
    all_to_all x1, blocking collectives, desk_derive(): small = all_to_all(x_new, axis_name=bus_axis, split_axis=0, concat_axis=0)  63.4 us
    all_to_all x1, waiting for transfers between devices, desk_derive(): small = all_to_all(x_new, axis_name=bus_axis, split_axis=0, concat_axis=0)  54.8 us
    all_to_all x1, blocking collectives, send_rows(): lax.all_to_all(desk_derive(values, 'expert'), 'dp', split_axis=1, concat_...  34.5 us
    unnamed x57, local copies, waits for them, and re-layouts  25.7 us
    scatter x2, local copies, waits for them, and re-layouts, slot_rank(): return jnp.zeros((count,), jnp.int32).at[order].set(within)  23.3 us
    all_to_all x1, waiting for transfers between devices, per_device(): lax.all_to_all(outgoing, 'expert', split_axis=1, concat_axis=1, tiled=True)  18.1 us
    all_to_all x1, waiting for transfers between devices, per_device(): lax.all_to_all(grads_out, 'expert', split_axis=1, concat_axis=1, tiled=True)  17.8 us
    scatter x2, local copies, waits for them, and re-layouts, per_device(): outgoing = jnp.zeros((cap_expert, expert_count, model_width), jnp.bfloat1...  17.1 us
  transfers between devices with their start and end apart: 9, of which 7 were waited for; matrix products, arithmetic and copies ran while one was open for 20% of the time, Pallas kernels for 0%

profile of v1, /device:TPU:0, one launch (start us, length us, event | category | flops | bytes accessed | tf_op | source)
XLA Modules:
  0.0 553.4 jit_solution(3175806261251121657)
XLA Ops:
  8.1 5.0 sort.34
  13.1 11.8 %gather_fusion.2 = s32[2048]{0:T(1024)S(1)} fusion(s32[2048]{0:T(1024)S(1)} %reshape.289, s32[2048]{0:T(1024)S(1)} %get-tuple-element.259), kind=kCustom, calls=%fused_computation.2 | custom fusion | bytes 24576 | tf_op jit(solution)/shard_map/gather | solution.py:14
  25.0 9.0 %while.48 = (s32[]{:T(128)}, u32[32]{0:T(128)S(1)}, u32[32]{0:T(128)S(1)}, s32[2048]{0:T(1024)S(1)}, s32[]{:T(128)}, /*index=5*/s32[]{:T(128)}, s32[]{}) while((s32[]{:T(128)}, u32[32]{0:T(128)S(1)}, u32[32]{0:T(128)S(1)}, s32[2048]{0:T(1024)S(1)}, s32[]{:T(128)}, /*index=5*/s32[]{:T(128)}, s32[]{}) %tuple.152), condition=%wide.region_2.3_spmd.clone, body=%wide.region_1.2_spmd.clone.sunk | while | flops 1444 | bytes 5732 | solution.py:15
  40.5 15.8 %select_subtract_fusion = s32[2048]{0:T(1024)S(1)} fusion(pred[2048]{0:T(1024)(128)(4,1)S(1)} %get-tuple-element.214, pred[2048]{0:T(1024)(128)(4,1)S(1)} %get-tuple-element.213, pred[2048]{0:T(1024)(128)(4,1)S(1)} %get-tuple-element.212, pred[2048]{0:T(1024)(128)(4,1)S(1)} %get-tuple-element.211, pred[2048]{0:T(1024)(128)(4,1)S(1)} %get-tuple-element.210, ...), kind=kLoop, calls=%fused_computation.164 | loop fusion | flops 53248 | bytes 67684 | tf_op jit(solution)/shard_map/sub | solution.py:16
  56.2 8.0 %scatter_custom_fusion = s32[2048]{0:T(1024)S(1)} fusion(s32[2048]{0:T(1024)S(1)} %get-tuple-element.260, s32[2048]{0:T(1024)S(1)} %select_subtract_fusion, s32[]{:T(128)} %constant.134.clone.1), kind=kCustom, calls=%fused_computation.189 | custom fusion | bytes 8196 | tf_op jit(solution)/shard_map/scatter | solution.py:17
  65.4 8.1 %scatter_custom_fusion.5 = s32[2592]{0:T(1024)S(1)} fusion(s32[2048]{0:T(1024)S(1)} %get-tuple-element.262, s32[2048]{0:T(1024)S(1)} %get-tuple-element.307, s32[]{:T(128)} %constant.134.clone.1), kind=kCustom, calls=%fused_computation.175 | custom fusion | bytes 10372
  73.6 11.8 %all_to_all.50 = s32[81,4,8]{0,1,2:T(4,128)S(1)} all-to-all(s32[81,4,8]{0,1,2:T(4,128)S(1)} %copy.246), channel_id=1, replica_groups=mesh['dp'=4,'expert'=8] {'expert'}, dimensions={2} | all-to-all | bytes 20736 | tf_op jit(solution)/shard_map/all_to_all | solution.py:22
  94.8 7.6 %gather_fusion.3 = f32[2592,256]{1,0:T(8,128)} fusion(f32[1024,256]{1,0:T(8,128)S(1)} %bitcast.199, s32[3072]{0:T(1024)S(1)} %pad_clamp_fusion.2), kind=kCustom, calls=%fused_computation.3 | custom fusion | bytes 5318784 | tf_op jit(solution)/shard_map/gather | solution.py:74
  102.4 10.7 %fusion.107 = (f32[81,4,1,256]{3,2,1,0:T(1,128)S(1)}, f32[81,4,1,256]{3,2,1,0:T(1,128)S(1)}, f32[81,4,1,256]{3,2,1,0:T(1,128)S(1)}, f32[81,4,1,256]{3,2,1,0:T(1,...) fusion(f32[81,4,8,256]{3,2,1,0:T(8,128)} %bitcast.215), kind=kLoop, calls=%fused_computation.228 | loop fusion | bytes 5308416 | tf_op jit(solution)/shard_map/split | solution.py:34
  130.4 54.8 %all-to-all-done.2 = f32[8,81,4,1,256]{4,2,3,1,0:T(4,128)} async-done(((f32[8,81,4,1,256]{4,2,3,1,0:T(4,128)}), f32[8,81,4,1,256]{4,2,3,1,0:T(4,128)}, u32[]{:S(2)}, u32[]{:S(2)}) %all-to-all-start.2) | async-done | bytes 2654240 | tf_op jit(solution)/shard_map/all_to_all | solution.py:36
  193.7 6.3 %while.49 = (s32[]{:T(128)}, u32[8]{0:T(128)S(1)}, u32[8]{0:T(128)S(1)}, s32[256]{0:T(256)S(1)}, s32[]{:T(128)}, /*index=5*/s32[]{:T(128)}, s32[]{}) while((s32[]{:T(128)}, u32[8]{0:T(128)S(1)}, u32[8]{0:T(128)S(1)}, s32[256]{0:T(256)S(1)}, s32[]{:T(128)}, /*index=5*/s32[]{:T(128)}, s32[]{}) %tuple.155), condition=%wide.region_8.9_spmd.clone, body=%wide.region_7.8_spmd.clone.sunk | while | flops 1132 | bytes 4580 | solution.py:15
  206.0 15.3 %scatter_custom_fusion.1 = s32[256]{0:T(256)S(1)} fusion(s32[256]{0:T(256)S(1)} %compare_select_fusion.22, s32[256]{0:T(256)S(1)} %select_subtract_fusion.1, s32[]{:T(128)} %constant.134.clone.1), kind=kCustom, calls=%fused_computation.220 | custom fusion | bytes 1028 | tf_op jit(solution)/shard_map/scatter | solution.py:17
  230.0 8.4 %gather_fusion.4 = f32[2048,256]{1,0:T(8,128)S(1)} fusion(f32[2592,256]{1,0:T(8,128)} %bitcast.200, s32[2048]{0:T(1024)S(1)} %get-tuple-element.257), kind=kCustom, calls=%fused_computation.4 | custom fusion | bytes 4202496 | tf_op jit(solution)/shard_map/gather | solution.py:76
  244.3 16.0 %scatter_fusion = bf16[33,8,1024]{2,1,0:T(8,128)(2,1)S(1)} fusion(bf16[33,8,1024]{2,1,0:T(8,128)(2,1)S(1)} %broadcast.283.clone, s32[256]{0:T(256)S(1)} %bitcast.203, bf16[256,1024]{1,0:T(8,128)(2,1)S(1)} %gather_fusion.6), kind=kCustom, calls=%fused_computation.12 | custom fusion | bytes 1574912 | tf_op jit(solution)/shard_map/scatter | solution.py:89
  266.1 18.1 %all-to-all-done.4 = bf16[33,8,1024]{2,0,1:T(8,128)(2,1)S(1)} async-done(((bf16[33,8,1024]{2,0,1:T(8,128)(2,1)}), bf16[33,8,1024]{2,0,1:T(8,128)(2,1)S(1)}, u32[]{:S(2)}, u32[]{:S(2)}) %all-to-all-start.4) | async-done | bytes 540704 | tf_op jit(solution)/shard_map/all_to_all | solution.py:91
  301.5 13.0 %all-to-all-done.5 = bf16[33,8,1024]{2,0,1:T(8,128)(2,1)S(1)} async-done(((bf16[33,8,1024]{2,0,1:T(8,128)(2,1)}), bf16[33,8,1024]{2,0,1:T(8,128)(2,1)S(1)}, u32[]{:S(2)}, u32[]{:S(2)}) %all-to-all-start.5) | async-done | bytes 540704 | tf_op jit(solution)/shard_map/all_to_all | solution.py:98
  327.6 16.0 %scatter_fusion.1 = bf16[33,8,1024]{2,1,0:T(8,128)(2,1)S(1)} fusion(bf16[33,8,1024]{2,1,0:T(8,128)(2,1)S(1)} %broadcast.283, s32[256]{0:T(256)S(1)} %bitcast.204, bf16[256,1024]{1,0:T(8,128)(2,1)S(1)} %reshape.473), kind=kCustom, calls=%fused_computation.13 | custom fusion | bytes 1574912 | tf_op jit(solution)/shard_map/scatter | solution.py:130
  348.5 17.8 %all-to-all-done.6 = bf16[33,8,1024]{2,0,1:T(8,128)(2,1)S(1)} async-done(((bf16[33,8,1024]{2,0,1:T(8,128)(2,1)}), bf16[33,8,1024]{2,0,1:T(8,128)(2,1)S(1)}, u32[]{:S(2)}, u32[]{:S(2)}) %all-to-all-start.6) | async-done | bytes 540704 | tf_op jit(solution)/shard_map/all_to_all | solution.py:132
  366.4 6.4 %fusion.40 = bf16[33,8,1024]{2,1,0:T(8,128)(2,1)S(1)} fusion(bf16[1,1024,2048]{2,1,0:T(8,128)(2,1)} %all-gather.5.cloned.1.call-done, bf16[1,2048,1024]{2,1,0:T(8,128)(2,1)} %all-gather.7.cloned.1.call-done, bf16[264,2048]{1,0:T(8,128)(2,1)} %copy-done.16, bf16[33,8,1024]{2,0,1:T(8,128)(2,1)S(1)} %all-to-all-done.6), kind=kOutput, calls=%fused_computation.55 | convolution fusion | flops 2216484864 | bytes 10551296 | tf_op jit(solution)/shard_map/dot_general | solution.py:139
  383.1 12.4 %all-to-all-done.7 = bf16[33,8,1024]{2,0,1:T(8,128)(2,1)S(1)} async-done(((bf16[33,8,1024]{2,0,1:T(8,128)(2,1)}), bf16[33,8,1024]{2,0,1:T(8,128)(2,1)S(1)}, u32[]{:S(2)}, u32[]{:S(2)}) %all-to-all-start.7) | async-done | bytes 540704 | tf_op jit(solution)/shard_map/all_to_all | solution.py:143
  405.1 12.1 %scatter_custom_fusion.6 = f32[2592,256]{1,0:T(8,128)} fusion(s32[2048]{0:T(1024)} %get-tuple-element.261, f32[2048,256]{1,0:T(8,128)S(1)} %reshape.306, f32[]{:T(128)} %constant.151.clone.1, pred[2048]{0:T(1024)(128)(4,1)S(1)} %lt.149), kind=kCustom, calls=%fused_computation.45 | custom fusion | flops 524288 | bytes 4754432
  427.9 63.4 %all_to_all.51 = f32[8,81,4,1,256]{4,2,1,3,0:T(4,128)S(1)} all-to-all(f32[8,81,4,1,256]{4,2,1,3,0:T(4,128)S(1)} %copy.277), channel_id=1, replica_groups=mesh['dp'=4,'expert'=8] {'expert'}, dimensions={0} | all-to-all | bytes 5308416 | tf_op jit(solution)/shard_map/all_to_all | solution.py:36
  491.8 34.5 %all_to_all.52 = f32[81,4,8,256]{3,2,0,1:T(8,128)S(1)} all-to-all(f32[81,4,8,256]{3,2,0,1:T(8,128)S(1)} %copy.278), channel_id=1, replica_groups=mesh['dp'=4,'expert'=8] {'dp'}, dimensions={1} | all-to-all | bytes 5308416 | tf_op jit(solution)/shard_map/all_to_all | solution.py:39
  528.2 16.1 %scatter_custom_fusion.4 = f32[1024,256]{1,0:T(8,128)S(1)} fusion(s32[2592]{0:T(1024)S(1)} %fusion.76, f32[2592,256]{1,0:T(8,128)} %bitcast.218, f32[]{:T(128)} %constant.151.clone.1), kind=kCustom, calls=%fused_computation.73 | custom fusion | flops 663552 | bytes 1049088 | tf_op jit(solution)/shard_map/scatter-add | solution.py:164
  (260 shorter events, 154.6 us)
Async XLA Ops:
  7.2 289.7 %copy-start = (bf16[2,1024,8]{1,2,0:T(8,128)(2,1)S(1)}, bf16[2,1024,8]{1,2,0:T(8,128)(2,1)}, u32[]{:S(2)}) copy-start(bf16[2,1024,8]{1,2,0:T(8,128)(2,1)} %param.24) | copy-start | bytes 98308
  24.9 39.4 %copy-start.8 = (s32[128,16]{0,1:T(8,128)S(1)}, s32[128,16]{0,1:T(8,128)}, u32[]{:S(2)}) copy-start(s32[128,16]{0,1:T(8,128)} %param.18) | copy-start | bytes 24580
  24.9 39.6 %copy-start.15 = (s32[2]{0:T(128)S(1)}, s32[2]{0:T(128)}, u32[]{:S(2)}) copy-start(s32[2]{0:T(128)} %constant.166) | copy-start | bytes 28
  24.9 39.7 %copy-start.13 = (s32[2]{0:T(128)S(1)}, s32[2]{0:T(128)}, u32[]{:S(2)}) copy-start(s32[2]{0:T(128)} %constant.163) | copy-start | bytes 28
  25.0 39.7 %copy-start.14 = (s32[2]{0:T(128)S(1)}, s32[2]{0:T(128)}, u32[]{:S(2)}) copy-start(s32[2]{0:T(128)} %constant.169) | copy-start | bytes 28
  25.0 69.8 %copy-start.1 = (f32[4,256,256]{2,1,0:T(8,128)S(1)}, f32[4,256,256]{2,1,0:T(8,128)}, u32[]{:S(2)}) copy-start(f32[4,256,256]{2,1,0:T(8,128)} %param.15) | copy-start | bytes 3145732
  86.0 8.4 %all-to-all-start.1 = ((s32[81,4,8]{0,2,1:T(8,128)}), s32[81,4,8]{0,2,1:T(8,128)S(1)}, u32[]{:S(2)}, u32[]{:S(2)}) async-start(s32[81,4,8]{0,2,1:T(8,128)} %copy.247), calls=%async_computation.1 | async-start | bytes 32768 | tf_op jit(solution)/shard_map/all_to_all | solution.py:21
  89.7 176.4 %all-gather.5.cloned.1.call-start = ((), (), s32[]{:S(2)}) async-start(), calls=%async_computation.10 | async-start | bytes 5242880 | tf_op jit(solution)/shard_map/all_gather | solution.py:62
  119.6 5.4 copy-start.5
  119.6 65.6 %all-to-all-start.2 = ((f32[8,81,4,1,256]{4,2,3,1,0:T(4,128)}), f32[8,81,4,1,256]{4,2,3,1,0:T(4,128)}, u32[]{:S(2)}, u32[]{:S(2)}) async-start(f32[8,81,4,1,256]{4,2,3,1,0:T(4,128)} %fusion.67), calls=%async_computation.2 | async-start | bytes 5308416 | tf_op jit(solution)/shard_map/all_to_all | solution.py:36
  124.2 163.7 %all-gather.7.cloned.1.call-start = ((), (), s32[]{:S(2)}) async-start(), calls=%async_computation.11 | async-start | bytes 5242880 | tf_op jit(solution)/shard_map/all_gather | solution.py:63
  189.0 37.2 %all-to-all-start.3 = ((f32[81,4,8,256]{3,2,0,1:T(8,128)}), f32[81,4,8,256]{3,2,0,1:T(8,128)}, u32[]{:S(2)}, u32[]{:S(2)}) async-start(f32[81,4,8,256]{3,2,0,1:T(8,128)} %copy.257), calls=%async_computation.3 | async-start | bytes 5308416 | tf_op jit(solution)/shard_map/all_to_all | solution.py:39
  193.7 6.5 %copy-start.11 = (s32[4,128]{1,0:T(4,128)S(1)}, s32[4,128]{1,0:T(4,128)}, u32[]{:S(2)}) copy-start(s32[4,128]{1,0:T(4,128)} %param.19) | copy-start | bytes 6148
  261.5 22.8 %all-to-all-start.4 = ((bf16[33,8,1024]{2,0,1:T(8,128)(2,1)}), bf16[33,8,1024]{2,0,1:T(8,128)(2,1)S(1)}, u32[]{:S(2)}, u32[]{:S(2)}) async-start(bf16[33,8,1024]{2,0,1:T(8,128)(2,1)} %copy.263), calls=%async_computation.4 | async-start | bytes 1310720 | tf_op jit(solution)/shard_map/all_to_all | solution.py:91
  287.9 3.9 copy-start.16
  292.9 21.6 %all-to-all-start.5 = ((bf16[33,8,1024]{2,0,1:T(8,128)(2,1)}), bf16[33,8,1024]{2,0,1:T(8,128)(2,1)S(1)}, u32[]{:S(2)}, u32[]{:S(2)}) async-start(bf16[33,8,1024]{2,0,1:T(8,128)(2,1)} %copy.265), calls=%async_computation.5 | async-start | bytes 1310720 | tf_op jit(solution)/shard_map/all_to_all | solution.py:98
  317.5 3.0 copy-start.4
  317.8 2.8 copy-start.3
  317.8 3.6 copy-start.12
  344.7 21.6 %all-to-all-start.6 = ((bf16[33,8,1024]{2,0,1:T(8,128)(2,1)}), bf16[33,8,1024]{2,0,1:T(8,128)(2,1)S(1)}, u32[]{:S(2)}, u32[]{:S(2)}) async-start(bf16[33,8,1024]{2,0,1:T(8,128)(2,1)} %copy.273), calls=%async_computation.6 | async-start | bytes 1310720 | tf_op jit(solution)/shard_map/all_to_all | solution.py:132
  373.9 21.6 %all-to-all-start.7 = ((bf16[33,8,1024]{2,0,1:T(8,128)(2,1)}), bf16[33,8,1024]{2,0,1:T(8,128)(2,1)S(1)}, u32[]{:S(2)}, u32[]{:S(2)}) async-start(bf16[33,8,1024]{2,0,1:T(8,128)(2,1)} %copy.275), calls=%async_computation.7 | async-start | bytes 1310720 | tf_op jit(solution)/shard_map/all_to_all | solution.py:143
  377.7 5.4 copy-start.7
  417.3 8.5 %copy-start.2 = (f32[2592,256]{1,0:T(8,128)S(1)}, f32[2592,256]{1,0:T(8,128)}, u32[]{:S(2)}) copy-start(f32[2592,256]{1,0:T(8,128)} %scatter_custom_fusion.6) | copy-start | bytes 7962628
  528.2 16.4 %copy-start.10 = (f32[4,256]{1,0:T(4,128)S(1)}, f32[4,256]{1,0:T(4,128)}, u32[]{:S(2)}) copy-start(f32[4,256]{1,0:T(4,128)} %param.16) | copy-start | bytes 12292
  (2 other events, 1.2 us)
Sparse Core Ops, SparseCore 0:
  92.3 51.1 all-gather.4
  145.4 68.2 all-gather.6
